TPU v7x, 32 devices: a whole 2x2x4 slice. The times are simulated.
32 devices in a mesh: lat: 8 (over z, core), lon: 4 (over y, x).
Axes of the slice: x: 2, y: 2, z: 4, core: 2. Of those that a mesh axis runs over, the one named last changes fastest.
Arguments:
- predicted_state: float32 [1440, 13312], P('lon', 'lat'), may hold values from -24 to 24
- verified_state: float32 [1440, 13312], P('lon', 'lat'), may hold values from -20 to 20
- normal_state: float32 [1440, 13312], P('lon', 'lat'), may hold values from -3 to 3
Outputs:
- energy_curves: float32 [3, 52, 721], replicated
- rms_error: float32 [52], replicated
- anomaly_corr: float32 [52], replicated
All inputs are finite; a program needn't handle non-finite values.
Results may differ from a plain program's by a relative error of at most 0.00005.
Values sent between devices are 32-bit elements; how exact they have to be, the bound alone decides.
A program may use at most 64 MiB of HBM per device.

v0:
```python
import jax
import jax.numpy as jnp
from jax import lax
from jax.sharding import PartitionSpec as P

FIELDS = 52
epsilon = 1e-06


def latitude_weights(lat_index, parallel_number):
    return jnp.cos(jnp.pi * ((lat_index.astype(jnp.float32) + 0.5) / parallel_number - 0.5))


def dft_table(lon_rows, lon_total, wave_count):
    longitudes = jnp.arange(lon_rows, dtype=jnp.int32)
    waves = jnp.arange(wave_count, dtype=jnp.int32)
    phase = longitudes[:, None] * waves[None, :] % lon_total
    angle = 2.0 * jnp.pi / lon_total * phase.astype(jnp.float32)
    return jnp.concatenate([jnp.cos(angle), -jnp.sin(angle)], axis=1)


def transform_columns(stacked, table):
    return lax.dot_general(
        stacked,
        table,
        (((0,), (0,)), ((), ())),
        precision=lax.Precision.HIGHEST,
        preferred_element_type=jnp.float32,
    )


def row_powers(fore_coeffs, true_coeffs, wave_count):
    diff_coeffs = fore_coeffs - true_coeffs

    def square(coeffs):
        return (
            coeffs[:, :wave_count] * coeffs[:, :wave_count]
            + coeffs[:, wave_count:] * coeffs[:, wave_count:]
        )

    return jnp.stack([square(fore_coeffs), square(true_coeffs), square(diff_coeffs)], axis=1)


def local(predicted_state, verified_state, normal_state):
    quantity_labels = FIELDS
    meridian_lines, meridian_number = predicted_state.shape
    parallel_lines = meridian_number // quantity_labels
    parallel_number = parallel_lines * lax.axis_size("lat")
    lon_devices = lax.axis_size("lon")
    lon_total = meridian_lines * lon_devices
    wave_count = lon_total // 2 + 1
    row_share = meridian_number // lon_devices
    lat_first = lax.axis_index("lat") * parallel_lines
    weights = latitude_weights(
        lat_first + jnp.arange(parallel_lines, dtype=jnp.int32), parallel_number
    )
    weight_total = jnp.sum(
        latitude_weights(jnp.arange(parallel_number, dtype=jnp.int32), parallel_number)
    )
    predicted_block = predicted_state.reshape(meridian_lines, parallel_lines, quantity_labels)
    observed_block = verified_state.reshape(meridian_lines, parallel_lines, quantity_labels)
    normal_block = normal_state.reshape(meridian_lines, parallel_lines, quantity_labels)
    mismatch_parts = predicted_block - observed_block
    predicted_anomalies = predicted_block - normal_block
    observed_anomalies = observed_block - normal_block
    broad_layout = weights[None, :, None]
    skill_terms = jnp.stack(
        [
            jnp.sum(broad_layout * mismatch_parts * mismatch_parts, axis=(0, 1)),
            jnp.sum(broad_layout * predicted_anomalies * observed_anomalies, axis=(0, 1)),
            jnp.sum(broad_layout * predicted_anomalies * predicted_anomalies, axis=(0, 1)),
            jnp.sum(broad_layout * observed_anomalies * observed_anomalies, axis=(0, 1)),
        ]
    )
    predicted_meridians = predicted_block.transpose(0, 2, 1).reshape(
        meridian_lines, meridian_number
    )
    true_cols = observed_block.transpose(0, 2, 1).reshape(meridian_lines, meridian_number)
    full_table = dft_table(lon_total, lon_total, wave_count)
    fore_blocks = predicted_meridians.reshape(meridian_lines, lon_devices, row_share)
    true_blocks = true_cols.reshape(meridian_lines, lon_devices, row_share)
    fore_part = lax.all_to_all(fore_blocks, "lon", split_axis=1, concat_axis=0, tiled=True)[:, 0, :]
    true_part = lax.all_to_all(true_blocks, "lon", split_axis=1, concat_axis=0, tiled=True)[:, 0, :]
    items = fore_part.shape[1]
    stacked = jnp.concatenate([fore_part, true_part], axis=1)
    coeffs = transform_columns(stacked, full_table)
    powers = row_powers(coeffs[:items], coeffs[items:], wave_count)
    share_start = lax.axis_index("lon") * row_share
    global_cols = share_start + jnp.arange(row_share, dtype=jnp.int32)
    field_of = global_cols // parallel_lines
    row_weights = latitude_weights(lat_first + global_cols % parallel_lines, parallel_number)
    row_scale = row_weights / (lon_total * lon_total * weight_total)
    weighted = powers.reshape(row_share, 3 * wave_count) * row_scale[:, None]
    field_index = jnp.arange(quantity_labels, dtype=jnp.int32)
    window = min(quantity_labels, row_share // parallel_lines + 2)
    first_field = share_start // parallel_lines
    window_index = jnp.arange(window, dtype=jnp.int32)
    offset = field_of - first_field
    selector = (offset[None, :] == window_index[:, None]).astype(jnp.float32)
    band_sum = jnp.dot(
        selector, weighted, precision=lax.Precision.HIGHEST, preferred_element_type=jnp.float32
    )
    band_sum = lax.psum(band_sum, "lat")
    gathered = lax.all_gather(band_sum, "lon", axis=0, tiled=True)
    slot_index = jnp.arange(lon_devices * window, dtype=jnp.int32)
    slot_field = slot_index // window * row_share // parallel_lines + slot_index % window
    placer = (slot_field[None, :] == field_index[:, None]).astype(jnp.float32)
    summed = jnp.dot(
        placer, gathered, precision=lax.Precision.HIGHEST, preferred_element_type=jnp.float32
    )
    energy_curves = summed.reshape(quantity_labels, 3, wave_count).transpose(1, 0, 2)
    skill_means = lax.psum(skill_terms, ("lat", "lon")) / (lon_total * weight_total)
    rms_error = jnp.sqrt(skill_means[0])
    anomaly_corr = skill_means[1] / jnp.sqrt(
        (skill_means[2] + epsilon) * (skill_means[3] + epsilon)
    )
    return (energy_curves, rms_error, anomaly_corr)


def solution(mesh):
    in_specs = (P("lon", "lat"), P("lon", "lat"), P("lon", "lat"))
    out_specs = (P(), P(), P())
    return jax.shard_map(local, mesh=mesh, in_specs=in_specs, out_specs=out_specs, check_vma=False)
```

profile of v0, /device:TPU:8, one launch (start us, length us, event | category | flops | bytes accessed | tf_op | source)
XLA Modules:
  0.0 275.4 jit_solution(18060614692774121550)
XLA Ops:
  7.2 3.2 %copy.26 = f32[360,1664]{0,1:T(8,128)} copy(f32[360,1664]{1,0:T(8,128)} %param.4) | data formatting | bytes 4792320 | tf_op args[1]
  10.4 2.4 reshape.125
  12.8 1.9 copy.27
  14.8 4.8 %all-to-all-start.1 = ((f32[360,4,416]{0,2,1:T(8,128)}), f32[360,4,416]{0,2,1:T(8,128)}, u32[]{:S(2)}, u32[]{:S(2)}) async-start(f32[360,4,416]{0,2,1:T(8,128)} %bitcast.41), calls=%async_computation.1 | async-start | bytes 5111808 | tf_op jit(solution)/shard_map/all_to_all | solution.py:83
  19.6 2.2 copy.23
  21.7 2.4 reshape.124
  24.2 2.1 copy.24
  26.5 23.2 %all-to-all-done.1 = f32[360,4,416]{0,2,1:T(8,128)} async-done(((f32[360,4,416]{0,2,1:T(8,128)}), f32[360,4,416]{0,2,1:T(8,128)}, u32[]{:S(2)}, u32[]{:S(2)}) %all-to-all-start.1) | async-done | bytes 2396192 | tf_op jit(solution)/shard_map/all_to_all | solution.py:83
  49.7 3.6 %all-to-all-start = ((f32[360,4,416]{0,2,1:T(8,128)}), f32[360,4,416]{0,2,1:T(8,128)S(1)}, u32[]{:S(2)}, u32[]{:S(2)}) async-start(f32[360,4,416]{0,2,1:T(8,128)} %bitcast.39), calls=%async_computation | async-start | bytes 5111808 | tf_op jit(solution)/shard_map/all_to_all | solution.py:82
  53.4 4.3 %fusion.17 = (f32[1664]{0:T(1024)S(1)}, f32[1664]{0:T(1024)S(1)}, f32[1664]{0:T(1024)S(1)}, f32[1664]{0:T(1024)S(1)}) fusion(f32[360,1664]{1,0:T(8,128)} %param.3, f32[360,1664]{1,0:T(8,128)} %param.4, f32[1664]{0:T(1024)S(1)} %mul.171, f32[360,1664]{1,0:T(8,128)} %param.5), kind=kLoop, calls=%fused_computation.26 | loop fusion | flops 8379904 | bytes 7221760 | tf_op jit(solution)/shard_map/reduce_sum | solution.py:69
  60.1 55.8 %psum.15 = f32[4,52]{1,0:T(4,128)S(1)} all-reduce(f32[4,52]{1,0:T(4,128)S(1)} %pad_maximum_fusion.1), channel_id=1, replica_groups=mesh['lat'=8,'lon'=4] {'lat','lon'}, use_global_device_ids=true, to_apply=%region_10.11 | all-reduce | flops 208 | bytes 1664 | tf_op jit(solution)/shard_map/psum | solution.py:112
  116.5 19.7 %sine_negate_fusion = (f32[1440,721]{1,0:T(8,128)}, f32[1440,721]{1,0:T(8,128)}) fusion(), kind=kLoop, calls=%fused_computation.12 | loop fusion | flops 10382400 | bytes 8305920 | tf_op jit(solution)/shard_map/neg | solution.py:19
  136.2 4.8 %copy.28 = f32[4,360,1,416]{1,0,3,2:T(4,128)} copy(f32[4,360,1,416]{1,3,0,2:T(8,128)} %bitcast.7) | data formatting | bytes 4792320 | tf_op jit(solution)/shard_map/all_to_all | solution.py:83
  141.1 4.0 %squeeze.5 = f32[1440,416]{0,1:T(8,128)} reshape(f32[4,360,1,416]{1,0,3,2:T(4,128)} %copy.28) | data formatting | bytes 4792320 | tf_op jit(solution)/shard_map/squeeze | solution.py:83
  145.1 3.1 %copy.25 = f32[4,360,1,416]{1,0,3,2:T(4,128)} copy(f32[4,360,1,416]{1,3,0,2:T(8,128)S(1)} %bitcast.40) | data formatting | bytes 4792320 | tf_op jit(solution)/shard_map/all_to_all | solution.py:82
  148.2 4.2 %squeeze.4 = f32[1440,416]{0,1:T(8,128)} reshape(f32[4,360,1,416]{1,0,3,2:T(4,128)} %copy.25) | data formatting | bytes 4792320 | tf_op jit(solution)/shard_map/squeeze | solution.py:82
  152.4 29.4 %fusion = f32[832,1442]{1,0:T(8,128)S(1)} fusion(f32[1440,721]{1,0:T(8,128)} %get-tuple-element.20, f32[1440,721]{1,0:T(8,128)} %get-tuple-element.21, f32[1440,416]{0,1:T(8,128)S(1)} %copy-done.1, f32[1440,416]{0,1:T(8,128)} %squeeze.4), kind=kOutput, calls=%fused_computation | convolution fusion | flops 20734851072 | bytes 17897216 | tf_op jit(solution)/shard_map/dot_general | solution.py:23
  183.4 2.1 pad_maximum_fusion
  185.5 5.6 %copy.29 = f32[416,3,721]{0,2,1:T(8,128)} copy(f32[416,3,721]{2,0,1:T(8,128)} %pad_maximum_fusion) | data formatting | bytes 7198464 | tf_op jit(solution)/shard_map/stack | solution.py:41
  191.1 4.9 %reshape.126 = f32[416,2163]{0,1:T(8,128)} reshape(f32[416,3,721]{0,2,1:T(8,128)} %copy.29) | data formatting | bytes 7198464 | tf_op jit(solution)/shard_map/reshape | solution.py:93
  196.0 5.2 %fusion.7 = f32[15,2163]{1,0:T(8,128)} fusion(f32[416,2163]{0,1:T(8,128)} %reshape.126, f32[416]{0:T(512)S(1)} %fusion.37, s32[416]{0:T(512)S(1)} %fusion.29), kind=kOutput, calls=%fused_computation.8 | convolution fusion | flops 162871488 | bytes 3732340 | tf_op jit(solution)/shard_map/dot_general | solution.py:100
  201.2 54.4 %all-reduce.2.cloned.1.call-done = f32[15,2163]{1,0:T(8,128)} async-done(((f32[15,2163]{1,0:T(8,128)}), f32[15,2163]{1,0:T(8,128)}) %all-reduce.2.cloned.1.call-update) | async-done | bytes 129796 | tf_op jit(solution)/shard_map/psum | solution.py:103
  255.6 11.1 %all-gather = f32[4,15,2163]{2,1,0:T(8,128)S(1)} all-gather(f32[1,15,2163]{2,1,0:T(8,128)} %bitcast.43), channel_id=1, replica_groups=mesh['lat'=8,'lon'=4] {'lon'}, dimensions={0}, use_global_device_ids=true | all-gather | bytes 648900 | tf_op jit(solution)/shard_map/all_gather | solution.py:104
  267.7 0.9 copy.30
  (31 shorter events, 4.5 us)
Async XLA Ops:
  14.8 4.8 %copy-start = (f32[360,1664]{1,0:T(8,128)S(1)}, f32[360,1664]{1,0:T(8,128)}, u32[]{:S(2)}) copy-start(f32[360,1664]{1,0:T(8,128)} %param.3) | copy-start | bytes 7188484
  14.8 34.9 %all-to-all-start.1 = ((f32[360,4,416]{0,2,1:T(8,128)}), f32[360,4,416]{0,2,1:T(8,128)}, u32[]{:S(2)}, u32[]{:S(2)}) async-start(f32[360,4,416]{0,2,1:T(8,128)} %bitcast.41), calls=%async_computation.1 | async-start | bytes 5111808 | tf_op jit(solution)/shard_map/all_to_all | solution.py:83
  49.7 95.4 %all-to-all-start = ((f32[360,4,416]{0,2,1:T(8,128)}), f32[360,4,416]{0,2,1:T(8,128)S(1)}, u32[]{:S(2)}, u32[]{:S(2)}) async-start(f32[360,4,416]{0,2,1:T(8,128)} %bitcast.39), calls=%async_computation | async-start | bytes 5111808 | tf_op jit(solution)/shard_map/all_to_all | solution.py:82
  53.3 202.3 %all-reduce.2.cloned.1.call-start = ((), (), s32[]{:S(2)}) async-start(), calls=%async_computation.2 | async-start | bytes 278528 | tf_op jit(solution)/shard_map/psum | solution.py:103
  148.2 4.2 %copy-start.1 = (f32[1440,416]{0,1:T(8,128)S(1)}, f32[1440,416]{0,1:T(8,128)}, u32[]{:S(2)}) copy-start(f32[1440,416]{0,1:T(8,128)} %squeeze.5) | copy-start | bytes 7188484
Sparse Core Ops, SparseCore 0:
  201.3 54.3 all-reduce.1
where the time goes:
time: 276 us; the launch traced here: 275 us
  waiting for transfers between devices  77.7 us (28%)
  blocking collectives  66.9 us (24%)
  local copies, waits for them, and re-layouts  42.9 us (16%)
  matrix products  35 us (13%)
  other arithmetic  29 us (11%)
  between operations  15.5 us (6%)
  starting transfers between devices  8.44 us (3%)
    psum x1, blocking collectives, local(): lax.psum(skill_terms, ('lat', 'lon')) / (lon_total * weight_total)  55.8 us
    psum x1, waiting for transfers between devices, local(): band_sum = lax.psum(band_sum, 'lat')  54.4 us
    dot_general x1, matrix products, transform_columns(): lax.dot_general(stacked, table, (((0,), (0,)), ((), ())), precision=lax.P...  29.4 us
    all_to_all x1, waiting for transfers between devices, local(): lax.all_to_all(true_blocks, 'lon', split_axis=1, concat_axis=0, tiled=True)  23.2 us
    neg x1, other arithmetic, dft_table(): return jnp.concatenate([jnp.cos(angle), -jnp.sin(angle)], axis=1)  19.7 us
    all_gather x1, blocking collectives, local(): gathered = lax.all_gather(band_sum, 'lon', axis=0, tiled=True)  11.1 us
    unnamed x8, local copies, waits for them, and re-layouts  6.34 us
    another operation x1, local copies, waits for them, and re-layouts, row_powers(): jnp.stack([square(fore_coeffs), square(true_coeffs), square(diff_coeffs)]...  5.61 us
  transfers between devices with their start and end apart: 3, of which 2 were waited for; matrix products, arithmetic and copies ran while one was open for 15% of the time, Pallas kernels for 0%

commit v1 on v0

--- a/solution.py
+++ b/solution.py
@@ -1,3 +1,4 @@
+import functools
 import jax
 import jax.numpy as jnp
 from jax import lax
@@ -5,6 +6,15 @@
 
 FIELDS = 52
 epsilon = 1e-06
+
+
+def define_records(mat, across, along_axis):
+    for b in (along_axis, across):
+        mat = lax.psum(mat, axis_name=b)
+    return mat
+
+
+scenes_name = functools.partial(define_records, across="lon", along_axis="lat")
 
 
 def latitude_weights(lat_index, parallel_number):
@@ -109,7 +119,7 @@
         placer, gathered, precision=lax.Precision.HIGHEST, preferred_element_type=jnp.float32
     )
     energy_curves = summed.reshape(quantity_labels, 3, wave_count).transpose(1, 0, 2)
-    skill_means = lax.psum(skill_terms, ("lat", "lon")) / (lon_total * weight_total)
+    skill_means = scenes_name(skill_terms) / (lon_total * weight_total)
     rms_error = jnp.sqrt(skill_means[0])
     anomaly_corr = skill_means[1] / jnp.sqrt(
         (skill_means[2] + epsilon) * (skill_means[3] + epsilon)

time: 276 us -> 246 us (0.89)
  blocking collectives: 66.9 us -> 36.7 us
    psum x1 -> x2, blocking collectives: 55.8 us -> 25.6 us  [define_records(): mat = lax.psum(mat, axis_name=b)]
  transfers between devices with their start and end apart: 3 -> 3, of which waited for: 2 -> 2; matrix products, arithmetic and copies ran while one was open for 15% -> 17% of each run, Pallas kernels for 0% -> 0%
where the time goes in v1:
time: 246 us; the launch traced here: 245 us
  waiting for transfers between devices  77.9 us (32%)
  local copies, waits for them, and re-layouts  42.9 us (17%)
  blocking collectives  36.7 us (15%)
  matrix products  35 us (14%)
  other arithmetic  29 us (12%)
  between operations  15.5 us (6%)
  starting transfers between devices  8.44 us (3%)
    psum x1, waiting for transfers between devices, local(): band_sum = lax.psum(band_sum, 'lat')  54.7 us
    dot_general x1, matrix products, transform_columns(): lax.dot_general(stacked, table, (((0,), (0,)), ((), ())), precision=lax.P...  29.4 us
    psum x2, blocking collectives, define_records(): mat = lax.psum(mat, axis_name=b)  25.6 us
    all_to_all x1, waiting for transfers between devices, local(): lax.all_to_all(true_blocks, 'lon', split_axis=1, concat_axis=0, tiled=True)  23.2 us
    neg x1, other arithmetic, dft_table(): return jnp.concatenate([jnp.cos(angle), -jnp.sin(angle)], axis=1)  19.7 us
    all_gather x1, blocking collectives, local(): gathered = lax.all_gather(band_sum, 'lon', axis=0, tiled=True)  11.1 us
    unnamed x8, local copies, waits for them, and re-layouts  6.34 us
    another operation x1, local copies, waits for them, and re-layouts, row_powers(): jnp.stack([square(fore_coeffs), square(true_coeffs), square(diff_coeffs)]...  5.61 us
  transfers between devices with their start and end apart: 3, of which 2 were waited for; matrix products, arithmetic and copies ran while one was open for 17% of the time, Pallas kernels for 0%

profile of v1, /device:TPU:8, one launch (start us, length us, event | category | flops | bytes accessed | tf_op | source)
XLA Modules:
  0.0 245.4 jit_solution(3181763924175955648)
XLA Ops:
  7.2 3.2 %copy.26 = f32[360,1664]{0,1:T(8,128)} copy(f32[360,1664]{1,0:T(8,128)} %param.4) | data formatting | bytes 4792320 | tf_op args[1]
  10.4 2.4 reshape.125
  12.8 1.9 copy.27
  14.8 4.8 %all-to-all-start.1 = ((f32[360,4,416]{0,2,1:T(8,128)}), f32[360,4,416]{0,2,1:T(8,128)}, u32[]{:S(2)}, u32[]{:S(2)}) async-start(f32[360,4,416]{0,2,1:T(8,128)} %bitcast.41), calls=%async_computation.1 | async-start | bytes 5111808 | tf_op jit(solution)/shard_map/all_to_all | solution.py:93
  19.6 2.2 copy.23
  21.7 2.4 reshape.124
  24.2 2.1 copy.24
  26.5 23.2 %all-to-all-done.1 = f32[360,4,416]{0,2,1:T(8,128)} async-done(((f32[360,4,416]{0,2,1:T(8,128)}), f32[360,4,416]{0,2,1:T(8,128)}, u32[]{:S(2)}, u32[]{:S(2)}) %all-to-all-start.1) | async-done | bytes 2396192 | tf_op jit(solution)/shard_map/all_to_all | solution.py:93
  49.7 3.6 %all-to-all-start = ((f32[360,4,416]{0,2,1:T(8,128)}), f32[360,4,416]{0,2,1:T(8,128)S(1)}, u32[]{:S(2)}, u32[]{:S(2)}) async-start(f32[360,4,416]{0,2,1:T(8,128)} %bitcast.39), calls=%async_computation | async-start | bytes 5111808 | tf_op jit(solution)/shard_map/all_to_all | solution.py:92
  53.4 4.3 %fusion.17 = (f32[1664]{0:T(1024)S(1)}, f32[1664]{0:T(1024)S(1)}, f32[1664]{0:T(1024)S(1)}, f32[1664]{0:T(1024)S(1)}) fusion(f32[360,1664]{1,0:T(8,128)} %param.3, f32[360,1664]{1,0:T(8,128)} %param.4, f32[1664]{0:T(1024)S(1)} %mul.171, f32[360,1664]{1,0:T(8,128)} %param.5), kind=kLoop, calls=%fused_computation.26 | loop fusion | flops 8379904 | bytes 7221760 | tf_op jit(solution)/shard_map/reduce_sum | solution.py:79
  60.1 12.2 %psum.22 = f32[4,52]{1,0:T(4,128)S(1)} all-reduce(f32[4,52]{1,0:T(4,128)S(1)} %pad_maximum_fusion.1), channel_id=1, replica_groups=mesh['lat'=8,'lon'=4] {'lat'}, use_global_device_ids=true, to_apply=%region_10.11 | all-reduce | flops 208 | bytes 1664 | tf_op jit(solution)/shard_map/psum | solution.py:13
  72.4 13.4 %psum.23 = f32[4,52]{1,0:T(4,128)S(1)} all-reduce(f32[4,52]{1,0:T(4,128)S(1)} %psum.22), channel_id=1, replica_groups=mesh['lat'=8,'lon'=4] {'lon'}, use_global_device_ids=true, to_apply=%region_11.12 | all-reduce | flops 208 | bytes 1664 | tf_op jit(solution)/shard_map/psum | solution.py:13
  86.4 19.7 %sine_negate_fusion = (f32[1440,721]{1,0:T(8,128)}, f32[1440,721]{1,0:T(8,128)}) fusion(), kind=kLoop, calls=%fused_computation.12 | loop fusion | flops 10382400 | bytes 8305920 | tf_op jit(solution)/shard_map/neg | solution.py:29
  106.0 4.8 %copy.28 = f32[4,360,1,416]{1,0,3,2:T(4,128)} copy(f32[4,360,1,416]{1,3,0,2:T(8,128)} %bitcast.7) | data formatting | bytes 4792320 | tf_op jit(solution)/shard_map/all_to_all | solution.py:93
  110.9 4.0 %squeeze.5 = f32[1440,416]{0,1:T(8,128)} reshape(f32[4,360,1,416]{1,0,3,2:T(4,128)} %copy.28) | data formatting | bytes 4792320 | tf_op jit(solution)/shard_map/squeeze | solution.py:93
  114.9 3.1 %copy.25 = f32[4,360,1,416]{1,0,3,2:T(4,128)} copy(f32[4,360,1,416]{1,3,0,2:T(8,128)S(1)} %bitcast.40) | data formatting | bytes 4792320 | tf_op jit(solution)/shard_map/all_to_all | solution.py:92
  118.0 4.2 %squeeze.4 = f32[1440,416]{0,1:T(8,128)} reshape(f32[4,360,1,416]{1,0,3,2:T(4,128)} %copy.25) | data formatting | bytes 4792320 | tf_op jit(solution)/shard_map/squeeze | solution.py:92
  122.2 29.4 %fusion = f32[832,1442]{1,0:T(8,128)S(1)} fusion(f32[1440,721]{1,0:T(8,128)} %get-tuple-element.20, f32[1440,721]{1,0:T(8,128)} %get-tuple-element.21, f32[1440,416]{0,1:T(8,128)S(1)} %copy-done.1, f32[1440,416]{0,1:T(8,128)} %squeeze.4), kind=kOutput, calls=%fused_computation | convolution fusion | flops 20734851072 | bytes 17897216 | tf_op jit(solution)/shard_map/dot_general | solution.py:33
  153.2 2.1 pad_maximum_fusion
  155.3 5.6 %copy.29 = f32[416,3,721]{0,2,1:T(8,128)} copy(f32[416,3,721]{2,0,1:T(8,128)} %pad_maximum_fusion) | data formatting | bytes 7198464 | tf_op jit(solution)/shard_map/stack | solution.py:51
  160.9 4.9 %reshape.126 = f32[416,2163]{0,1:T(8,128)} reshape(f32[416,3,721]{0,2,1:T(8,128)} %copy.29) | data formatting | bytes 7198464 | tf_op jit(solution)/shard_map/reshape | solution.py:103
  165.8 5.2 %fusion.7 = f32[15,2163]{1,0:T(8,128)} fusion(f32[416,2163]{0,1:T(8,128)} %reshape.126, f32[416]{0:T(512)S(1)} %fusion.37, s32[416]{0:T(512)S(1)} %fusion.29), kind=kOutput, calls=%fused_computation.8 | convolution fusion | flops 162871488 | bytes 3732340 | tf_op jit(solution)/shard_map/dot_general | solution.py:110
  171.0 54.7 %all-reduce.2.cloned.1.call-done = f32[15,2163]{1,0:T(8,128)} async-done(((f32[15,2163]{1,0:T(8,128)}), f32[15,2163]{1,0:T(8,128)}) %all-reduce.2.cloned.1.call-update) | async-done | bytes 129796 | tf_op jit(solution)/shard_map/psum | solution.py:113
  225.7 11.1 %all-gather = f32[4,15,2163]{2,1,0:T(8,128)S(1)} all-gather(f32[1,15,2163]{2,1,0:T(8,128)} %bitcast.43), channel_id=1, replica_groups=mesh['lat'=8,'lon'=4] {'lon'}, dimensions={0}, use_global_device_ids=true | all-gather | bytes 648900 | tf_op jit(solution)/shard_map/all_gather | solution.py:114
  (32 shorter events, 5.4 us)
Async XLA Ops:
  14.8 4.8 %copy-start = (f32[360,1664]{1,0:T(8,128)S(1)}, f32[360,1664]{1,0:T(8,128)}, u32[]{:S(2)}) copy-start(f32[360,1664]{1,0:T(8,128)} %param.3) | copy-start | bytes 7188484
  14.8 34.9 %all-to-all-start.1 = ((f32[360,4,416]{0,2,1:T(8,128)}), f32[360,4,416]{0,2,1:T(8,128)}, u32[]{:S(2)}, u32[]{:S(2)}) async-start(f32[360,4,416]{0,2,1:T(8,128)} %bitcast.41), calls=%async_computation.1 | async-start | bytes 5111808 | tf_op jit(solution)/shard_map/all_to_all | solution.py:93
  49.7 65.3 %all-to-all-start = ((f32[360,4,416]{0,2,1:T(8,128)}), f32[360,4,416]{0,2,1:T(8,128)S(1)}, u32[]{:S(2)}, u32[]{:S(2)}) async-start(f32[360,4,416]{0,2,1:T(8,128)} %bitcast.39), calls=%async_computation | async-start | bytes 5111808 | tf_op jit(solution)/shard_map/all_to_all | solution.py:92
  53.3 172.4 %all-reduce.2.cloned.1.call-start = ((), (), s32[]{:S(2)}) async-start(), calls=%async_computation.2 | async-start | bytes 278528 | tf_op jit(solution)/shard_map/psum | solution.py:113
  118.0 4.2 %copy-start.1 = (f32[1440,416]{0,1:T(8,128)S(1)}, f32[1440,416]{0,1:T(8,128)}, u32[]{:S(2)}) copy-start(f32[1440,416]{0,1:T(8,128)} %squeeze.5) | copy-start | bytes 7188484
Sparse Core Ops, SparseCore 0:
  171.1 54.5 all-reduce.1
